TPU v7x, 256 devices: a whole 4x4x8 slice. The times are simulated.
256 devices in a mesh: seq: 64 (over y, z, core), tab: 4 (over x).
Axes of the slice: x: 4, y: 4, z: 8, core: 2. Of those that a mesh axis runs over, the one named last changes fastest.
Arguments:
- cotangent: bfloat16 [65536, 2560], P('seq', 'tab'), may hold values from -6 to 6
- saved_value: bfloat16 [65536, 2560], P('seq', 'tab'), may hold values from -6 to 6
- gate_scale: float32 [65536], P('seq'), may hold values from 0.2 to 1
- conv_weight: float32 [4, 2560], P(None, 'tab'), may hold values from -3 to 3
- value_weight: bfloat16 [1280, 2560], P(None, 'tab'), may hold values from -0.25 to 0.25
- owner_ids: int32 [8, 65536, 1], P('tab', 'seq'), may hold values from 0 to 63; in each aligned block of 1024 rows (0 to 1023, 1024 to 2047, ..., all dimensions but the last counted through in order) at most 64 rows name the same one
- local_row: int32 [8, 65536], P('tab', 'seq'), may hold values from 0 to 511
- row_table: float32 [8, 32768, 160], P('tab', 'seq'), may hold values from -6 to 6
- moment_one: float32 [8, 32768, 160], P('tab', 'seq'), may hold values from -6 to 6
- moment_two: float32 [8, 32768, 160], P('tab', 'seq'), may hold values from 0.5 to 4
Outputs:
- new_table: float32 [8, 32768, 160], P('tab', 'seq')
- new_first: float32 [8, 32768, 160], P('tab', 'seq')
- new_second: float32 [8, 32768, 160], P('tab', 'seq')
Inputs may be any that keep to these rules, and one draw needn't show every extreme that they name: `owner_ids`: within each aligned block of 1024 tokens of one head (one device's tokens), no owner is named by more than 64 tokens; in some blocks one owner is named by exactly 64.
All inputs are finite; a program needn't handle non-finite values.
Results may differ from a plain program's by a relative error of at most 0.0029.
Values may be sent and summed in bfloat16 or wider, within the bound.
No kernel may reach another device: no remote copies, remote signals or barrier semaphores. Data moves between devices by JAX's collectives and lax.ppermute only.
A program may use at most 128 MiB of HBM per device.

v0:
```python
import jax
import jax.numpy as jnp
from jax import lax
from jax.sharding import PartitionSpec as P

beta_one = 0.9
beta_two = 0.95
learn_rate = 0.01
adam_steps = 10.0
epsilon = 1e-08


def from_behind(block, axis, distance):
    devices = range(lax.axis_size(axis))
    route = [(i - distance, i) for i in devices if i - distance in devices]
    return lax.ppermute(block, axis, route)


def causal_mix(context, conv_weight, length):
    mix_total = jnp.zeros((length, context.shape[1]), jnp.float32)
    for tap_index in range(4):
        row_start = 9 - 3 * tap_index
        mix_total = (
            mix_total + conv_weight[tap_index][None, :] * context[row_start : row_start + length]
        )
    return mix_total


def conv_adjoint(upstream, mixed_conv):
    squashed = jax.nn.sigmoid(mixed_conv)
    return upstream * squashed * (1.0 + mixed_conv * (1.0 - squashed))


def shards(
    cotangent,
    saved_value,
    gate_scale,
    conv_weight,
    value_weight,
    owner_ids,
    local_row,
    row_table,
    moment_one,
    moment_two,
):
    length = cotangent.shape[0]
    head_local = row_table.shape[0]
    table_rows = row_table.shape[1]
    head_dim = row_table.shape[2]
    own_width = head_local * head_dim
    peer_count = lax.axis_size("seq")
    count_cap = 4 * length // peer_count
    upstream = cotangent.astype(jnp.float32)
    value_rows = saved_value.astype(jnp.float32)
    prior_rows = from_behind(saved_value[length - 9 :], "seq", 1)
    context = jnp.concatenate([prior_rows.astype(jnp.float32), value_rows], axis=0)
    conv_grad = conv_adjoint(upstream, causal_mix(context, conv_weight, length))
    following = from_behind(conv_grad[:9], "seq", -1)
    extended = jnp.concatenate([conv_grad, following], axis=0)
    value_grad = upstream
    for tap_index in range(4):
        row_start = 3 * tap_index
        value_grad = (
            value_grad + conv_weight[tap_index][None, :] * extended[row_start : row_start + length]
        )
    scaled = (gate_scale[:, None] * value_grad).astype(jnp.bfloat16)
    full_term = lax.dot_general(
        value_weight, scaled, (((1,), (1,)), ((), ())), preferred_element_type=jnp.float32
    )
    summed = lax.psum(full_term, "tab")
    memory_grad = lax.dynamic_slice_in_dim(summed, lax.axis_index("tab") * own_width, own_width, 0)
    heads_grad = jnp.swapaxes(memory_grad.reshape(head_local, head_dim, length), 1, 2)
    owners = owner_ids[:, :, 0]
    position = jnp.arange(length, dtype=jnp.int32)
    earlier = position[None, :] < position[:, None]
    same_owner = owners[:, :, None] == owners[:, None, :]
    slot_rank = jnp.sum((same_owner & earlier[None]).astype(jnp.int32), axis=2)
    slot_index = owners * count_cap + slot_rank
    head_ids = jnp.broadcast_to(jnp.arange(head_local, dtype=jnp.int32)[:, None], slot_index.shape)
    send_grad = (
        jnp.zeros((head_local, peer_count * count_cap, head_dim), jnp.float32)
        .at[head_ids, slot_index]
        .set(heads_grad)
    )
    send_rows = (
        jnp.zeros((head_local, peer_count * count_cap), jnp.int32)
        .at[head_ids, slot_index]
        .set(local_row + 1)
    )
    send_grad = send_grad.reshape(head_local, peer_count, count_cap, head_dim)
    send_rows = send_rows.reshape(head_local, peer_count, count_cap)
    grads_in = lax.all_to_all(send_grad, "seq", split_axis=1, concat_axis=1, tiled=True)
    rows_in = lax.all_to_all(send_rows, "seq", split_axis=1, concat_axis=1, tiled=True)
    item_count = grads_in.shape[0]
    flat_rows = rows_in.reshape(item_count, -1) - 1
    flat_grads = grads_in.reshape(item_count, -1, head_dim)
    item_ids = jnp.broadcast_to(jnp.arange(item_count, dtype=jnp.int32)[:, None], flat_rows.shape)
    target = jnp.where(flat_rows < 0, table_rows, flat_rows)
    summed_rows = (
        jnp.zeros((item_count, table_rows, head_dim), jnp.float32)
        .at[item_ids, target]
        .add(flat_grads, mode="drop")
    )
    row_hits = (
        jnp.zeros((item_count, table_rows), jnp.int32).at[item_ids, target].add(1, mode="drop")
    )
    row_grad, row_hits = (summed_rows, row_hits)
    touched = (row_hits > 0)[:, :, None]
    first_next = beta_one * moment_one + (1.0 - beta_one) * row_grad
    second_next = beta_two * moment_two + (1.0 - beta_two) * row_grad * row_grad
    update = (
        first_next
        / (1.0 - beta_one**adam_steps)
        / (jnp.sqrt(second_next / (1.0 - beta_two**adam_steps)) + epsilon)
    )
    table_next = row_table - learn_rate * update
    return (
        jnp.where(touched, table_next, row_table),
        jnp.where(touched, first_next, moment_one),
        jnp.where(touched, second_next, moment_two),
    )


def solution(mesh):
    in_specs = (
        P("seq", "tab"),
        P("seq", "tab"),
        P("seq"),
        P(None, "tab"),
        P(None, "tab"),
        P("tab", "seq", None),
        P("tab", "seq"),
        P("tab", "seq", None),
        P("tab", "seq", None),
        P("tab", "seq", None),
    )
    out_specs = (P("tab", "seq", None), P("tab", "seq", None), P("tab", "seq", None))
    return jax.shard_map(shards, mesh=mesh, in_specs=in_specs, out_specs=out_specs, check_vma=False)
```

profile of v0, /device:TPU:1, one launch (start us, length us, event | category | flops | bytes accessed | tf_op | source)
XLA Modules:
  0.0 436.1 jit_solution(14999547283841224572)
XLA Ops:
  7.2 0.9 slice.42
  8.1 4.9 %collective-permute-start = (bf16[9,640]{1,0:T(8,128)(2,1)S(1)}, bf16[9,640]{1,0:T(8,128)(2,1)S(1)}, u32[]{:S(2)}, u32[]{:S(2)}) collective-permute-start(bf16[9,640]{1,0:T(8,128)(2,1)S(1)} %slice.42), channel_id=1, source_target_pairs={{0,4},{4,8},{8,12},{12,16},{16,20},{20,24},{24,28},{28,32},{32,36}... | collective-permute-start | bytes 34568 | tf_op jit(solution)/shard_map/ppermute | solution.py:16
  13.0 0.9 slice_reduce_fusion.3
  13.9 1.5 convert_element_type.17
  15.5 2.1 fusion.2
  17.6 1.9 collective-permute-start.1
  19.5 3.4 collective-permute-done.1
  22.9 6.8 %convolution_bitcast_fusion = f32[1280,1024]{0,1:T(8,128)} fusion(bf16[1280,640]{1,0:T(8,128)(2,1)S(1)} %copy-done, bf16[1024,640]{1,0:T(8,128)(2,1)S(1)} %copy-done.2, f32[9,640]{1,0:T(8,128)S(1)} %collective-permute-done.1, f32[1024,640]{1,0:T(8,128)S(1)} %fusion.2, f32[640]{0:T(1024)S(1)} %get-tuple-element.23, f32[640]{0:T(1024)S(1)} %get-tuple-element.24, ...), kind=kOutput, calls=%fused_computation.5 | convolution fusion | flops 1686896640 | bytes 10850816 | tf_op jit(solution)/shard_map/dot_general | solution.py:67
  29.7 0.7 copy-done.4
  30.4 0.3 iota_compare_fusion
  30.7 1.9 convert_reduce_fusion
  32.9 8.1 %scatter_custom_fusion = s32[8192]{0:T(1024)S(1)} fusion(s32[2048]{0:T(1024)S(1)} %get-tuple-element.29, s32[2048]{0:T(1024)S(1)} %get-tuple-element.28, s32[]{:T(128)} %constant.19.clone.1), kind=kCustom, calls=%fused_computation.60 | custom fusion | bytes 32772
  41.1 0.7 reshape.147
  41.8 11.6 %all-to-all-start = ((s32[64,1,128]{2,1,0:T(1,128)}), s32[64,1,128]{2,1,0:T(1,128)S(1)}, u32[]{:S(2)}, u32[]{:S(2)}) async-start(s32[64,1,128]{2,1,0:T(1,128)} %reshape.147), calls=%async_computation | async-start | bytes 65536 | tf_op jit(solution)/shard_map/all_to_all | solution.py:93
  53.5 93.5 %all-reduce.2.cloned.1.call-done = f32[1280,1024]{0,1:T(8,128)} async-done(((f32[1280,1024]{0,1:T(8,128)}), f32[1280,1024]{0,1:T(8,128)}) %all-reduce.2.cloned.1.call-update) | async-done | bytes 5242896 | tf_op jit(solution)/shard_map/psum | solution.py:70
  146.9 2.1 constant_dynamic-slice_fusion
  149.0 0.5 copy.100
  149.5 1.8 copy.116
  151.3 13.2 %scatter_custom_fusion.2 = f32[8192,160]{1,0:T(8,128)} fusion(s32[2048]{0:T(1024)S(1)} %get-tuple-element.29, f32[2048,160]{1,0:T(8,128)} %bitcast.36, f32[]{:T(128)} %constant.26.clone.1), kind=kCustom, calls=%fused_computation.6 | custom fusion | bytes 5243392
  164.5 7.7 %copy.104 = f32[2,64,64,160]{3,2,0,1:T(8,128)} copy(f32[2,64,64,160]{3,2,1,0:T(8,128)} %bitcast.32) | data formatting | bytes 10485760 | tf_op jit(solution)/shard_map/reshape | solution.py:90
  172.2 11.2 %all-to-all-start.1 = ((f32[2,64,64,160]{3,2,0,1:T(8,128)}), f32[2,64,64,160]{3,2,0,1:T(8,128)}, u32[]{:S(2)}, u32[]{:S(2)}) async-start(f32[2,64,64,160]{3,2,0,1:T(8,128)} %copy.104), calls=%async_computation.1 | async-start | bytes 16777216 | tf_op jit(solution)/shard_map/all_to_all | solution.py:92
  183.4 0.5 broadcast.188
  183.9 0.7 reduce.20
  185.2 44.3 %scatter_custom_fusion.1 = s32[1024]{0:T(1024)S(1)} fusion(s32[8192]{0:T(1024)S(1)} %bitcast.40, s32[8192]{0:T(1024)S(1)} %broadcast.161, s32[]{:T(128)} %constant.19.clone.1), kind=kCustom, calls=%fused_computation.74 | custom fusion | flops 8192 | bytes 4100
  229.5 139.6 %all-to-all-done.1 = f32[2,64,64,160]{3,2,0,1:T(8,128)} async-done(((f32[2,64,64,160]{3,2,0,1:T(8,128)}), f32[2,64,64,160]{3,2,0,1:T(8,128)}, u32[]{:S(2)}, u32[]{:S(2)}) %all-to-all-start.1) | async-done | bytes 5242912 | tf_op jit(solution)/shard_map/all_to_all | solution.py:92
  369.1 7.7 %copy.119 = f32[2,64,64,160]{3,2,1,0:T(8,128)} copy(f32[2,64,64,160]{3,2,0,1:T(8,128)} %all-to-all-done.1) | data formatting | bytes 10485760 | tf_op jit(solution)/shard_map/reshape | solution.py:96
  376.8 44.9 %scatter_custom_fusion.3 = f32[1024,160]{1,0:T(8,128)S(1)} fusion(s32[8192]{0:T(1024)S(1)} %bitcast.41, f32[8192,160]{1,0:T(8,128)} %bitcast.33, f32[]{:T(128)} %constant.26.clone.1), kind=kCustom, calls=%fused_computation.48 | custom fusion | flops 1310720 | bytes 655872
  421.7 0.6 copy.120
  422.3 4.0 broadcast_select_fusion
  426.4 1.0 copy.113
  427.3 1.0 copy.114
  428.3 1.0 copy.115
  (49 shorter events, 1.0 us)
Async XLA Ops:
  7.2 15.8 %copy-start = (bf16[1280,640]{1,0:T(8,128)(2,1)S(1)}, bf16[1280,640]{1,0:T(8,128)(2,1)}, u32[]{:S(2)}) copy-start(bf16[1280,640]{1,0:T(8,128)(2,1)} %param.14) | copy-start | bytes 4915204
  7.2 8.3 %copy-start.2 = (bf16[1024,640]{1,0:T(8,128)(2,1)S(1)}, bf16[1024,640]{1,0:T(8,128)(2,1)}, u32[]{:S(2)}) copy-start(bf16[1024,640]{1,0:T(8,128)(2,1)} %param.10) | copy-start | bytes 3932164
  7.2 139.7 %all-reduce.2.cloned.1.call-start = ((), (), s32[]{:S(2)}) async-start(), calls=%async_computation.2 | async-start | bytes 10485760 | tf_op jit(solution)/shard_map/psum | solution.py:70
  8.1 7.3 %collective-permute-start = (bf16[9,640]{1,0:T(8,128)(2,1)S(1)}, bf16[9,640]{1,0:T(8,128)(2,1)S(1)}, u32[]{:S(2)}, u32[]{:S(2)}) collective-permute-start(bf16[9,640]{1,0:T(8,128)(2,1)S(1)} %slice.42), channel_id=1, source_target_pairs={{0,4},{4,8},{8,12},{12,16},{16,20},{20,24},{24,28},{28,32},{32,36}... | collective-permute-start | bytes 34568 | tf_op jit(solution)/shard_map/ppermute | solution.py:16
  15.5 7.5 %copy-start.10 = (f32[1024]{0:T(1024)S(1)}, f32[1024]{0:T(1024)}, u32[]{:S(2)}) copy-start(f32[1024]{0:T(1024)} %param.12) | copy-start | bytes 12292
  17.6 5.3 %collective-permute-start.1 = (f32[9,640]{1,0:T(8,128)S(1)}, f32[9,640]{1,0:T(8,128)S(1)}, u32[]{:S(2)}, u32[]{:S(2)}) collective-permute-start(f32[9,640]{1,0:T(8,128)S(1)} %slice.56), channel_id=1, source_target_pairs={{4,0},{8,4},{12,8},{16,12},{20,16},{24,20},{28,24},{32,28},{36,32}... | collective-permute-start | bytes 69128 | tf_op jit(solution)/shard_map/ppermute | solution.py:16
  29.7 0.7 copy-start.4
  29.7 2.9 copy-start.8
  29.7 3.0 copy-start.9
  29.7 3.1 copy-start.5
  41.8 130.3 %all-to-all-start = ((s32[64,1,128]{2,1,0:T(1,128)}), s32[64,1,128]{2,1,0:T(1,128)S(1)}, u32[]{:S(2)}, u32[]{:S(2)}) async-start(s32[64,1,128]{2,1,0:T(1,128)} %reshape.147), calls=%async_computation | async-start | bytes 65536 | tf_op jit(solution)/shard_map/all_to_all | solution.py:93
  172.2 12.7 %copy-start.7 = (s32[2]{0:T(128)S(1)}, s32[2]{0:T(128)}, u32[]{:S(2)}) copy-start(s32[2]{0:T(128)} %constant.63) | copy-start | bytes 28
  172.2 12.8 %copy-start.6 = (s32[2]{0:T(128)S(1)}, s32[2]{0:T(128)}, u32[]{:S(2)}) copy-start(s32[2]{0:T(128)} %constant.66) | copy-start | bytes 28
  172.2 196.9 %all-to-all-start.1 = ((f32[2,64,64,160]{3,2,0,1:T(8,128)}), f32[2,64,64,160]{3,2,0,1:T(8,128)}, u32[]{:S(2)}, u32[]{:S(2)}) async-start(f32[2,64,64,160]{3,2,0,1:T(8,128)} %copy.104), calls=%async_computation.1 | async-start | bytes 16777216 | tf_op jit(solution)/shard_map/all_to_all | solution.py:92
  376.8 45.5 %copy-start.3 = (f32[2,512,160]{1,2,0:T(8,128)S(1)}, f32[2,512,160]{1,2,0:T(8,128)}, u32[]{:S(2)}) copy-start(f32[2,512,160]{1,2,0:T(8,128)} %param.19) | copy-start | bytes 1966084
  422.3 6.9 %copy-start.1 = (bf16[1280,640]{1,0:T(8,128)(2,1)S(1)}, bf16[1280,640]{1,0:T(8,128)(2,1)}, u32[]{:S(2)}) copy-start(bf16[1280,640]{1,0:T(8,128)(2,1)} %param.14) | copy-start | bytes 4915204
Sparse Core Ops, SparseCore 0:
  29.9 117.0 all-reduce.1
where the time goes:
time: 437 us; the launch traced here: 436 us
  waiting for transfers between devices  236 us (54%)
  other arithmetic  100 us (23%)
  local copies, waits for them, and re-layouts  48.5 us (11%)
  starting transfers between devices  29.7 us (7%)
  between operations  14.4 us (3%)
  matrix products  6.78 us (2%)
    all_to_all x1, waiting for transfers between devices, shards(): lax.all_to_all(send_grad, 'seq', split_axis=1, concat_axis=1, tiled=True)  140 us
    psum x1, waiting for transfers between devices, shards(): summed = lax.psum(full_term, 'tab')  93.5 us
    unnamed x9, other arithmetic  89.7 us
    unnamed x32, local copies, waits for them, and re-layouts  25.7 us
    all_to_all x1, starting transfers between devices, shards(): lax.all_to_all(send_rows, 'seq', split_axis=1, concat_axis=1, tiled=True)  11.6 us
    all_to_all x1, starting transfers between devices, shards(): lax.all_to_all(send_grad, 'seq', split_axis=1, concat_axis=1, tiled=True)  11.2 us
  transfers between devices with their start and end apart: 5, of which 3 were waited for; matrix products, arithmetic and copies ran while one was open for 19% of the time, Pallas kernels for 0%

commit v1 on v0

--- a/solution.py
+++ b/solution.py
@@ -67,7 +67,9 @@
     full_term = lax.dot_general(
         value_weight, scaled, (((1,), (1,)), ((), ())), preferred_element_type=jnp.float32
     )
-    summed = lax.psum(full_term, "tab")
+    summed = full_term
+    for hop in (1, 2):
+        summed = summed + lax.ppermute(summed, "tab", [(dev, dev ^ hop) for dev in range(4)])
     memory_grad = lax.dynamic_slice_in_dim(summed, lax.axis_index("tab") * own_width, own_width, 0)
     heads_grad = jnp.swapaxes(memory_grad.reshape(head_local, head_dim, length), 1, 2)
     owners = owner_ids[:, :, 0]

time: 437 us -> 538 us (1.23)
  waiting for transfers between devices: 236 us -> 343 us
  between operations: 14.4 us -> 1.02 us
  starting transfers between devices: 29.7 us -> 37.9 us
  other arithmetic: 100 us -> 106 us
    ppermute x0 -> x2, waiting for transfers between devices: none -> 200 us  [shards(): lax.ppermute(summed, 'tab', [(dev, dev ^ hop) for dev in range(4)])]
    psum x1 -> x0, waiting for transfers between devices: 93.5 us -> none  [shards(): summed = lax.psum(full_term, 'tab')]
    add x0 -> x2, other arithmetic: none -> 6.06 us  [shards(): summed + lax.ppermute(summed, 'tab', [(dev, dev ^ hop) for dev in range(4)])]
  transfers between devices with their start and end apart: 5 -> 6, of which waited for: 3 -> 4; matrix products, arithmetic and copies ran while one was open for 19% -> 16% of each run, Pallas kernels for 0% -> 0%
where the time goes in v1:
time: 538 us
  waiting for transfers between devices  343 us (64%)
  other arithmetic  106 us (20%)
  local copies, waits for them, and re-layouts  45.8 us (9%)
  starting transfers between devices  37.9 us (7%)
    ppermute x2, waiting for transfers between devices, shards(): lax.ppermute(summed, 'tab', [(dev, dev ^ hop) for dev in range(4)])  200 us
    all_to_all x1, waiting for transfers between devices, shards(): lax.all_to_all(send_grad, 'seq', split_axis=1, concat_axis=1, tiled=True)  140 us
    unnamed x9, other arithmetic  89.7 us
    unnamed x32, local copies, waits for them, and re-layouts  25 us
    all_to_all x1, starting transfers between devices, shards(): lax.all_to_all(send_grad, 'seq', split_axis=1, concat_axis=1, tiled=True)  13.6 us
    all_to_all x1, starting transfers between devices, shards(): lax.all_to_all(send_rows, 'seq', split_axis=1, concat_axis=1, tiled=True)  13.5 us
  transfers between devices with their start and end apart: 6, of which 4 were waited for; matrix products, arithmetic and copies ran while one was open for 16% of the time, Pallas kernels for 0%

profile of v1, /device:TPU:1, one launch (start us, length us, event | category | flops | bytes accessed | tf_op | source)
XLA Modules:
  0.0 537.6 jit_solution(14365454713520325662)
XLA Ops:
  0.7 0.9 slice.42
  1.5 4.9 collective-permute-start
  6.5 0.9 slice_reduce_fusion.3
  7.4 1.5 convert_element_type.17
  8.9 2.1 fusion.2
  11.0 1.9 collective-permute-start.1
  12.9 3.4 collective-permute-done.1
  16.3 3.4 convolution_bitcast_fusion
  19.7 1.3 collective-permute-start.2
  21.0 111.8 %collective-permute-done.2 = f32[1280,1024]{0,1:T(8,128)S(1)} collective-permute-done((f32[1280,1024]{0,1:T(8,128)S(1)}, f32[1280,1024]{0,1:T(8,128)S(1)}, u32[]{:S(2)}, u32[]{:S(2)}) %collective-permute-start.2) | collective-permute-done | bytes 5242912 | tf_op jit(solution)/shard_map/ppermute | solution.py:72
  132.9 3.0 add.107
  135.8 2.7 collective-permute-start.3
  138.9 1.9 convert_reduce_fusion
  141.0 8.1 %scatter_custom_fusion = s32[8192]{0:T(1024)S(1)} fusion(s32[2048]{0:T(1024)S(1)} %get-tuple-element.29, s32[2048]{0:T(1024)S(1)} %get-tuple-element.28, s32[]{:T(128)} %constant.19.clone.1), kind=kCustom, calls=%fused_computation.61 | custom fusion | bytes 32772
  149.3 0.7 reshape.147
  150.0 13.5 %all-to-all-start = ((s32[64,1,128]{2,1,0:T(1,128)}), s32[64,1,128]{2,1,0:T(1,128)S(1)}, u32[]{:S(2)}, u32[]{:S(2)}) async-start(s32[64,1,128]{2,1,0:T(1,128)} %reshape.147), calls=%async_computation | async-start | bytes 65536 | tf_op jit(solution)/shard_map/all_to_all | solution.py:95
  163.5 88.3 %collective-permute-done.3 = f32[1280,1024]{0,1:T(8,128)} collective-permute-done((f32[1280,1024]{0,1:T(8,128)}, f32[1280,1024]{0,1:T(8,128)}, u32[]{:S(2)}, u32[]{:S(2)}) %collective-permute-start.3) | collective-permute-done | bytes 5242912 | tf_op jit(solution)/shard_map/ppermute | solution.py:72
  251.8 3.1 dynamic-slice_add_fusion
  255.4 1.8 copy.116
  257.2 13.2 %scatter_custom_fusion.2 = f32[8192,160]{1,0:T(8,128)} fusion(s32[2048]{0:T(1024)S(1)} %get-tuple-element.29, f32[2048,160]{1,0:T(8,128)} %bitcast.36, f32[]{:T(128)} %constant.26.clone.1), kind=kCustom, calls=%fused_computation.6 | custom fusion | bytes 5243392
  270.4 7.7 %copy.104 = f32[2,64,64,160]{3,2,0,1:T(8,128)} copy(f32[2,64,64,160]{3,2,1,0:T(8,128)} %bitcast.32) | data formatting | bytes 10485760 | tf_op jit(solution)/shard_map/reshape | solution.py:92
  278.1 13.6 %all-to-all-start.1 = ((f32[2,64,64,160]{3,2,0,1:T(8,128)}), f32[2,64,64,160]{3,2,0,1:T(8,128)}, u32[]{:S(2)}, u32[]{:S(2)}) async-start(f32[2,64,64,160]{3,2,0,1:T(8,128)} %copy.104), calls=%async_computation.1 | async-start | bytes 16777216 | tf_op jit(solution)/shard_map/all_to_all | solution.py:94
  292.2 0.7 reduce.20
  293.5 44.3 %scatter_custom_fusion.1 = s32[1024]{0:T(1024)S(1)} fusion(s32[8192]{0:T(1024)S(1)} %bitcast.40, s32[8192]{0:T(1024)S(1)} %broadcast.161, s32[]{:T(128)} %constant.19.clone.1), kind=kCustom, calls=%fused_computation.75 | custom fusion | flops 8192 | bytes 4100
  337.9 139.6 %all-to-all-done.1 = f32[2,64,64,160]{3,2,0,1:T(8,128)} async-done(((f32[2,64,64,160]{3,2,0,1:T(8,128)}), f32[2,64,64,160]{3,2,0,1:T(8,128)}, u32[]{:S(2)}, u32[]{:S(2)}) %all-to-all-start.1) | async-done | bytes 5242912 | tf_op jit(solution)/shard_map/all_to_all | solution.py:94
  477.4 7.7 %copy.119 = f32[2,64,64,160]{3,2,1,0:T(8,128)} copy(f32[2,64,64,160]{3,2,0,1:T(8,128)} %all-to-all-done.1) | data formatting | bytes 10485760 | tf_op jit(solution)/shard_map/reshape | solution.py:98
  485.2 44.9 %scatter_custom_fusion.3 = f32[1024,160]{1,0:T(8,128)S(1)} fusion(s32[8192]{0:T(1024)S(1)} %bitcast.41, f32[8192,160]{1,0:T(8,128)} %bitcast.33, f32[]{:T(128)} %constant.26.clone.1), kind=kCustom, calls=%fused_computation.49 | custom fusion | flops 1310720 | bytes 655872
  530.1 0.6 copy.120
  530.6 4.0 broadcast_select_fusion
  534.7 1.0 copy.113
  535.7 1.0 copy.114
  536.6 1.0 copy.115
  (51 shorter events, 2.2 us)
Async XLA Ops:
  0.6 15.7 %copy-start = (bf16[1280,640]{1,0:T(8,128)(2,1)S(1)}, bf16[1280,640]{1,0:T(8,128)(2,1)}, u32[]{:S(2)}) copy-start(bf16[1280,640]{1,0:T(8,128)(2,1)} %param.14) | copy-start | bytes 4915204
  0.6 8.2 %copy-start.2 = (bf16[1024,640]{1,0:T(8,128)(2,1)S(1)}, bf16[1024,640]{1,0:T(8,128)(2,1)}, u32[]{:S(2)}) copy-start(bf16[1024,640]{1,0:T(8,128)(2,1)} %param.10) | copy-start | bytes 3932164
  1.5 7.3 %collective-permute-start = (bf16[9,640]{1,0:T(8,128)(2,1)S(1)}, bf16[9,640]{1,0:T(8,128)(2,1)S(1)}, u32[]{:S(2)}, u32[]{:S(2)}) collective-permute-start(bf16[9,640]{1,0:T(8,128)(2,1)S(1)} %slice.42), channel_id=1, source_target_pairs={{0,4},{4,8},{8,12},{12,16},{16,20},{20,24},{24,28},{28,32},{32,36}... | collective-permute-start | bytes 34568 | tf_op jit(solution)/shard_map/ppermute | solution.py:16
  8.9 7.4 %copy-start.10 = (f32[1024]{0:T(1024)S(1)}, f32[1024]{0:T(1024)}, u32[]{:S(2)}) copy-start(f32[1024]{0:T(1024)} %param.12) | copy-start | bytes 12292
  11.0 5.3 collective-permute-start.1
  19.7 118.9 %copy-start.4 = (s32[2,1024,1]{1,2,0:T(1,128)S(1)}, s32[2,1024,1]{1,2,0:T(1,128)}, u32[]{:S(2)}) copy-start(s32[2,1024,1]{1,2,0:T(1,128)} %param.15) | copy-start | bytes 24580
  19.7 121.1 %copy-start.8 = (s32[2]{0:T(128)S(1)}, s32[2]{0:T(128)}, u32[]{:S(2)}) copy-start(s32[2]{0:T(128)} %constant.57) | copy-start | bytes 28
  19.7 121.2 %copy-start.9 = (s32[2]{0:T(128)S(1)}, s32[2]{0:T(128)}, u32[]{:S(2)}) copy-start(s32[2]{0:T(128)} %constant.60) | copy-start | bytes 28
  19.7 121.3 %copy-start.5 = (s32[2,1024]{1,0:T(2,128)S(1)}, s32[2,1024]{1,0:T(2,128)}, u32[]{:S(2)}) copy-start(s32[2,1024]{1,0:T(2,128)} %param.16) | copy-start | bytes 24580
  19.7 113.1 %collective-permute-start.2 = (f32[1280,1024]{0,1:T(8,128)S(1)}, f32[1280,1024]{0,1:T(8,128)S(1)}, u32[]{:S(2)}, u32[]{:S(2)}) collective-permute-start(f32[1280,1024]{0,1:T(8,128)S(1)} %convolution_bitcast_fusion), channel_id=1, source_target_pairs={{0,1},{1,0},{2,3},{3,2},{4,5},{5,4},{6,7},{7,6},{8,9},{9,8},{10,11... | collective-permute-start | bytes 15728648 | tf_op jit(solution)/shard_map/ppermute | solution.py:72
  135.8 116.0 %collective-permute-start.3 = (f32[1280,1024]{0,1:T(8,128)}, f32[1280,1024]{0,1:T(8,128)}, u32[]{:S(2)}, u32[]{:S(2)}) collective-permute-start(f32[1280,1024]{0,1:T(8,128)} %add.107), channel_id=1, source_target_pairs={{0,2},{1,3},{2,0},{3,1},{4,6},{5,7},{6,4},{7,5},{8,10},{9,11},{10,... | collective-permute-start | bytes 15728648 | tf_op jit(solution)/shard_map/ppermute | solution.py:72
  150.0 128.1 %all-to-all-start = ((s32[64,1,128]{2,1,0:T(1,128)}), s32[64,1,128]{2,1,0:T(1,128)S(1)}, u32[]{:S(2)}, u32[]{:S(2)}) async-start(s32[64,1,128]{2,1,0:T(1,128)} %reshape.147), calls=%async_computation | async-start | bytes 65536 | tf_op jit(solution)/shard_map/all_to_all | solution.py:95
  278.1 15.1 %copy-start.7 = (s32[2]{0:T(128)S(1)}, s32[2]{0:T(128)}, u32[]{:S(2)}) copy-start(s32[2]{0:T(128)} %constant.63) | copy-start | bytes 28
  278.1 15.2 %copy-start.6 = (s32[2]{0:T(128)S(1)}, s32[2]{0:T(128)}, u32[]{:S(2)}) copy-start(s32[2]{0:T(128)} %constant.66) | copy-start | bytes 28
  278.1 199.3 %all-to-all-start.1 = ((f32[2,64,64,160]{3,2,0,1:T(8,128)}), f32[2,64,64,160]{3,2,0,1:T(8,128)}, u32[]{:S(2)}, u32[]{:S(2)}) async-start(f32[2,64,64,160]{3,2,0,1:T(8,128)} %copy.104), calls=%async_computation.1 | async-start | bytes 16777216 | tf_op jit(solution)/shard_map/all_to_all | solution.py:94
  485.2 45.5 %copy-start.3 = (f32[2,512,160]{1,2,0:T(8,128)S(1)}, f32[2,512,160]{1,2,0:T(8,128)}, u32[]{:S(2)}) copy-start(f32[2,512,160]{1,2,0:T(8,128)} %param.19) | copy-start | bytes 1966084
  530.6 6.9 %copy-start.1 = (bf16[1280,640]{1,0:T(8,128)(2,1)S(1)}, bf16[1280,640]{1,0:T(8,128)(2,1)}, u32[]{:S(2)}) copy-start(bf16[1280,640]{1,0:T(8,128)(2,1)} %param.14) | copy-start | bytes 4915204
